TPU v7x, 32 devices: a whole 2x2x4 slice. The times are simulated.
32 devices in a mesh: dp: 16 (over z, y, x), seq: 2 (over core).
Axes of the slice: x: 2, y: 2, z: 4, core: 2. Of those that a mesh axis runs over, the one named last changes fastest.
Arguments:
- tokens: bfloat16 [48, 512, 768], P('dp', 'seq'), may hold values from -6 to 6
- prev_logits: bfloat16 [48, 12, 512, 512], P('dp', None, 'seq'), may hold values from -6 to 6
- segment_ids: int32 [48, 512], P('dp'), may hold values from 0 to 5, never falling along the last dimension, each value on 1 to 192 neighbouring positions
- out_cotangent: bfloat16 [48, 512, 768], P('dp', 'seq'), may hold values from -6 to 6
- logit_cotangent: bfloat16 [48, 12, 512, 512], P('dp', None, 'seq'), may hold values from -0.59765625 to 0.59765625
- querymap: bfloat16 [768, 768], P(('dp', 'seq')), may hold values from -0.21875 to 0.21875
- querybias: bfloat16 [768], P(('dp', 'seq')), may hold values from -3 to 3
- keymap: bfloat16 [768, 768], P(('dp', 'seq')), may hold values from -0.21875 to 0.21875
- valuemap: bfloat16 [768, 768], P(('dp', 'seq')), may hold values from -0.21875 to 0.21875
- valuebias: bfloat16 [768], P(('dp', 'seq')), may hold values from -3 to 3
- mixmap: bfloat16 [768, 768], P(('dp', 'seq')), may hold values from -1.75 to 1.75
- mixbias: bfloat16 [768], P(('dp', 'seq')), may hold values from -3 to 3
- normgain: bfloat16 [768], P(('dp', 'seq')), may hold values from 0.5 to 1.5
- normbias: bfloat16 [768], P(('dp', 'seq')), may hold values from -3 to 3
- expandmap: bfloat16 [768, 3072], P(('dp', 'seq')), may hold values from -0.21875 to 0.21875
- expandbias: bfloat16 [3072], P(('dp', 'seq')), may hold values from -3 to 3
- shrinkmap: bfloat16 [3072, 768], P(('dp', 'seq')), may hold values from -0.109375 to 0.109375
- shrinkbias: bfloat16 [768], P(('dp', 'seq')), may hold values from -3 to 3
- outgain: bfloat16 [768], P(('dp', 'seq')), may hold values from 0.5 to 1.5
- outbias: bfloat16 [768], P(('dp', 'seq')), may hold values from -3 to 3
Outputs:
- layer_out: bfloat16 [48, 512, 768], P('dp', 'seq')
- raw_logits: bfloat16 [48, 12, 512, 512], P('dp', None, 'seq')
- tokens_grad: bfloat16 [48, 512, 768], P('dp', 'seq')
- logits_grad: bfloat16 [48, 12, 512, 512], P('dp', None, 'seq')
- querymap_grad: float32 [768, 768], P(('dp', 'seq'))
- querybias_grad: float32 [768], P(('dp', 'seq'))
- keymap_grad: float32 [768, 768], P(('dp', 'seq'))
- valuemap_grad: float32 [768, 768], P(('dp', 'seq'))
- valuebias_grad: float32 [768], P(('dp', 'seq'))
- mixmap_grad: float32 [768, 768], P(('dp', 'seq'))
- mixbias_grad: float32 [768], P(('dp', 'seq'))
- normgain_grad: float32 [768], P(('dp', 'seq'))
- normbias_grad: float32 [768], P(('dp', 'seq'))
- expandmap_grad: float32 [768, 3072], P(('dp', 'seq'))
- expandbias_grad: float32 [3072], P(('dp', 'seq'))
- shrinkmap_grad: float32 [3072, 768], P(('dp', 'seq'))
- shrinkbias_grad: float32 [768], P(('dp', 'seq'))
- outgain_grad: float32 [768], P(('dp', 'seq'))
- outbias_grad: float32 [768], P(('dp', 'seq'))
Inputs may be any that keep to these rules, and one draw needn't show every extreme that they name: `segment_ids`: along each row the ids never fall; each id covers 1 to 192 slots and in each row one covers exactly that many.
All inputs are finite; a program needn't handle non-finite values.
Results may differ from a plain program's by a relative error of at most 0.014.
Values may be sent and summed in bfloat16 or wider, within the bound.
A program may use at most 192 MiB of HBM per device.

v0:
```python
from functools import partial
import jax
import jax.numpy as jnp
from jax import lax
from jax.sharding import PartitionSpec as P

H = 12
HD = 64
norm_eps = 1e-06
mask_fill = -1e30


def matmul(left_side, right_side):
    return jnp.dot(left_side, right_side, preferred_element_type=jnp.float32)


def rows_product(left_side, right_side):
    return lax.dot_general(
        left_side, right_side, (((0,), (0,)), ((), ())), preferred_element_type=jnp.float32
    )


def cols_product(left_side, right_side):
    return lax.dot_general(
        left_side, right_side, (((1,), (1,)), ((), ())), preferred_element_type=jnp.float32
    )


def column_sum(matrix):
    return jnp.sum(matrix.astype(jnp.float32), 0)


def normalize(hidden):
    center = hidden - jnp.mean(hidden, -1, keepdims=True)
    scaled = lax.rsqrt(jnp.mean(center * center, -1, keepdims=True) + norm_eps)
    return (center * scaled, scaled)


def norm_back(upstream, unit_rows, scaled, gain_row):
    pulled = upstream * gain_row
    return scaled * (
        pulled
        - jnp.mean(pulled, -1, keepdims=True)
        - unit_rows * jnp.mean(pulled * unit_rows, -1, keepdims=True)
    )


def forward(shards, tokens, prev_logits, same_segment):
    (
        querymap,
        querybias,
        keymap,
        valuemap,
        valuebias,
        mixmap,
        mixbias,
        normgain,
        normbias,
        expandmap,
        expandbias,
        shrinkmap,
        shrinkbias,
        outgain,
        outbias,
    ) = shards
    weights = (
        lax.all_gather(querymap, ("dp", "seq"), axis=0, tiled=True),
        lax.all_gather(querybias, ("dp", "seq"), axis=0, tiled=True),
        lax.all_gather(keymap, ("dp", "seq"), axis=0, tiled=True),
        lax.all_gather(valuemap, ("dp", "seq"), axis=0, tiled=True),
        lax.all_gather(valuebias, ("dp", "seq"), axis=0, tiled=True),
        lax.all_gather(mixmap, ("dp", "seq"), axis=0, tiled=True),
        lax.all_gather(mixbias, ("dp", "seq"), axis=0, tiled=True),
        lax.all_gather(normgain, ("dp", "seq"), axis=0, tiled=True),
        lax.all_gather(normbias, ("dp", "seq"), axis=0, tiled=True),
        lax.all_gather(expandmap, ("dp", "seq"), axis=0, tiled=True),
        lax.all_gather(expandbias, ("dp", "seq"), axis=0, tiled=True),
        lax.all_gather(shrinkmap, ("dp", "seq"), axis=0, tiled=True),
        lax.all_gather(shrinkbias, ("dp", "seq"), axis=0, tiled=True),
        lax.all_gather(outgain, ("dp", "seq"), axis=0, tiled=True),
        lax.all_gather(outbias, ("dp", "seq"), axis=0, tiled=True),
    )
    (
        querymap,
        querybias,
        keymap,
        valuemap,
        valuebias,
        mixmap,
        mixbias,
        normgain,
        normbias,
        expandmap,
        expandbias,
        shrinkmap,
        shrinkbias,
        outgain,
        outbias,
    ) = weights
    seqrows, qlength, width = tokens.shape
    klength = prev_logits.shape[3]
    factor = HD ** (-0.5)
    token_rows = tokens.reshape(seqrows * qlength, width)
    queries = (matmul(token_rows, querymap) + querybias.astype(jnp.float32)).astype(jnp.bfloat16)
    keys_local = matmul(token_rows, keymap).astype(jnp.bfloat16)
    values_local = (matmul(token_rows, valuemap) + valuebias.astype(jnp.float32)).astype(
        jnp.bfloat16
    )
    keys_all, values_all = (
        lax.all_gather(keys_local.reshape(seqrows, qlength, width), "seq", axis=1, tiled=True),
        lax.all_gather(values_local.reshape(seqrows, qlength, width), "seq", axis=1, tiled=True),
    )
    query_heads = queries.reshape(seqrows, qlength, H, HD)
    key_heads = keys_all.reshape(seqrows, klength, H, HD)
    value_heads = values_all.reshape(seqrows, klength, H, HD)

    def attend(operands):
        query_one, key_one, value_one, prior_one, same_one = operands
        scores = jnp.einsum("qhe,khe->hqk", query_one, key_one, preferred_element_type=jnp.float32)
        logits = prior_one.astype(jnp.float32) + scores * factor
        masked = jnp.where(same_one, logits, mask_fill)
        row_peak = jnp.max(masked, -1, keepdims=True)
        exponent = jnp.exp(masked - row_peak)
        row_total = jnp.sum(exponent, -1, keepdims=True)
        attention = (exponent / row_total).astype(jnp.bfloat16)
        context = jnp.einsum(
            "hqk,khe->qhe", attention, value_one, preferred_element_type=jnp.float32
        )
        return (
            logits.astype(jnp.bfloat16),
            context.astype(jnp.bfloat16),
            row_peak + jnp.log(row_total),
        )

    raw_logits, context, log_total = lax.map(
        attend, (query_heads, key_heads, value_heads, prev_logits, same_segment)
    )
    context = context.reshape(seqrows * qlength, width)
    attended = matmul(context, mixmap) + mixbias.astype(jnp.float32)
    unit_first, scale_first = normalize(token_rows.astype(jnp.float32) + attended)
    normed = (unit_first * normgain.astype(jnp.float32) + normbias.astype(jnp.float32)).astype(
        jnp.bfloat16
    )
    inner_pre = matmul(normed, expandmap) + expandbias.astype(jnp.float32)
    active = jax.nn.gelu(inner_pre, approximate=False).astype(jnp.bfloat16)
    second = normed.astype(jnp.float32) + (
        matmul(active, shrinkmap) + shrinkbias.astype(jnp.float32)
    )
    unit_second, scale_second = normalize(second)
    layer_out = unit_second * outgain.astype(jnp.float32) + outbias.astype(jnp.float32)
    return (
        weights,
        queries,
        key_heads,
        value_heads,
        log_total,
        context,
        unit_first,
        scale_first,
        normed,
        inner_pre,
        active,
        unit_second,
        scale_second,
        raw_logits,
        layer_out,
    )


def body(
    tokens,
    prev_logits,
    segment_ids,
    out_cotangent,
    logit_cotangent,
    querymap,
    querybias,
    keymap,
    valuemap,
    valuebias,
    mixmap,
    mixbias,
    normgain,
    normbias,
    expandmap,
    expandbias,
    shrinkmap,
    shrinkbias,
    outgain,
    outbias,
):
    shards = (
        querymap,
        querybias,
        keymap,
        valuemap,
        valuebias,
        mixmap,
        mixbias,
        normgain,
        normbias,
        expandmap,
        expandbias,
        shrinkmap,
        shrinkbias,
        outgain,
        outbias,
    )
    seqrows, qlength, width = tokens.shape
    klength = segment_ids.shape[1]
    factor = HD ** (-0.5)
    own_segment = lax.dynamic_slice_in_dim(segment_ids, lax.axis_index("seq") * qlength, qlength, 1)
    same_segment = (own_segment[:, :, None] == segment_ids[:, None, :])[:, None]
    first_pass = forward(shards, tokens, prev_logits, same_segment)
    fenced = lax.optimization_barrier((shards, tokens, prev_logits, same_segment, first_pass[14]))
    state = forward(fenced[0], fenced[1], fenced[2], fenced[3])
    (
        weights,
        queries,
        key_heads,
        value_heads,
        log_total,
        context,
        unit_first,
        scale_first,
        normed,
        inner_pre,
        active,
        unit_second,
        scale_second,
        unused_logits,
        unused_output,
    ) = state
    raw_logits = first_pass[13]
    layer_out = first_pass[14]
    (
        querymap,
        querybias,
        keymap,
        valuemap,
        valuebias,
        mixmap,
        mixbias,
        normgain,
        normbias,
        expandmap,
        expandbias,
        shrinkmap,
        shrinkbias,
        outgain,
        outbias,
    ) = weights
    token_rows = tokens.reshape(seqrows * qlength, width)
    upstream = out_cotangent.reshape(seqrows * qlength, width).astype(jnp.float32)
    outgain_grad = jnp.sum(upstream * unit_second, 0)
    outbias_grad = jnp.sum(upstream, 0)
    second_grad = norm_back(upstream, unit_second, scale_second, outgain.astype(jnp.float32))
    branch_grad = second_grad.astype(jnp.bfloat16)
    shrinkbias_grad = column_sum(branch_grad)
    shrinkmap_grad = rows_product(active, branch_grad)
    active_grad = cols_product(branch_grad, shrinkmap)
    unused_value, gelu_pull = jax.vjp(partial(jax.nn.gelu, approximate=False), inner_pre)
    inner_grad = gelu_pull(active_grad)[0].astype(jnp.bfloat16)
    expandbias_grad = column_sum(inner_grad)
    expandmap_grad = rows_product(normed, inner_grad)
    normed_grad = second_grad + cols_product(inner_grad, expandmap)
    normgain_grad = jnp.sum(normed_grad * unit_first, 0)
    normbias_grad = jnp.sum(normed_grad, 0)
    first_grad = norm_back(normed_grad, unit_first, scale_first, normgain.astype(jnp.float32))
    attended_grad = first_grad.astype(jnp.bfloat16)
    mixbias_grad = column_sum(attended_grad)
    mixmap_grad = rows_product(context, attended_grad)
    context_grad = (
        cols_product(attended_grad, mixmap).astype(jnp.bfloat16).reshape(seqrows, qlength, H, HD)
    )
    query_heads = queries.reshape(seqrows, qlength, H, HD)

    def attend_back(operands):
        (
            query_one,
            key_one,
            value_one,
            prior_one,
            same_one,
            total_one,
            upstream_one,
            cotangent_one,
        ) = operands
        scores = jnp.einsum("qhe,khe->hqk", query_one, key_one, preferred_element_type=jnp.float32)
        logits = prior_one.astype(jnp.float32) + scores * factor
        attention = jnp.exp(jnp.where(same_one, logits, mask_fill) - total_one)
        prob_grad = jnp.einsum(
            "qhe,khe->hqk", upstream_one, value_one, preferred_element_type=jnp.float32
        )
        row_dot = jnp.sum(prob_grad * attention, -1, keepdims=True)
        logit_grad = (cotangent_one.astype(jnp.float32) + attention * (prob_grad - row_dot)).astype(
            jnp.bfloat16
        )
        query_part = (
            jnp.einsum("hqk,khe->qhe", logit_grad, key_one, preferred_element_type=jnp.float32)
            * factor
        )
        key_part = (
            jnp.einsum("hqk,qhe->khe", logit_grad, query_one, preferred_element_type=jnp.float32)
            * factor
        )
        value_part = jnp.einsum(
            "hqk,qhe->khe",
            attention.astype(jnp.bfloat16),
            upstream_one,
            preferred_element_type=jnp.float32,
        )
        return (logit_grad, query_part, key_part, value_part)

    logits_grad, query_grad, key_partial, value_partial = lax.map(
        attend_back,
        (
            query_heads,
            key_heads,
            value_heads,
            prev_logits,
            same_segment,
            log_total,
            context_grad,
            logit_cotangent,
        ),
    )
    key_grad, value_grad = (
        lax.psum_scatter(
            key_partial.reshape(seqrows, klength, width).astype(jnp.bfloat16),
            "seq",
            scatter_dimension=1,
            tiled=True,
        ).astype(jnp.float32),
        lax.psum_scatter(
            value_partial.reshape(seqrows, klength, width).astype(jnp.bfloat16),
            "seq",
            scatter_dimension=1,
            tiled=True,
        ).astype(jnp.float32),
    )
    query_grad = query_grad.reshape(seqrows * qlength, width).astype(jnp.bfloat16)
    key_grad = key_grad.reshape(seqrows * qlength, width).astype(jnp.bfloat16)
    value_grad = value_grad.reshape(seqrows * qlength, width).astype(jnp.bfloat16)
    querymap_grad = rows_product(token_rows, query_grad)
    querybias_grad = column_sum(query_grad)
    keymap_grad = rows_product(token_rows, key_grad)
    valuemap_grad = rows_product(token_rows, value_grad)
    valuebias_grad = column_sum(value_grad)
    tokens_grad = (
        first_grad
        + cols_product(query_grad, querymap)
        + cols_product(key_grad, keymap)
        + cols_product(value_grad, valuemap)
    )
    owned = (
        lax.psum_scatter(querymap_grad, ("dp", "seq"), scatter_dimension=0, tiled=True),
        lax.psum_scatter(querybias_grad, ("dp", "seq"), scatter_dimension=0, tiled=True),
        lax.psum_scatter(keymap_grad, ("dp", "seq"), scatter_dimension=0, tiled=True),
        lax.psum_scatter(valuemap_grad, ("dp", "seq"), scatter_dimension=0, tiled=True),
        lax.psum_scatter(valuebias_grad, ("dp", "seq"), scatter_dimension=0, tiled=True),
        lax.psum_scatter(mixmap_grad, ("dp", "seq"), scatter_dimension=0, tiled=True),
        lax.psum_scatter(mixbias_grad, ("dp", "seq"), scatter_dimension=0, tiled=True),
        lax.psum_scatter(normgain_grad, ("dp", "seq"), scatter_dimension=0, tiled=True),
        lax.psum_scatter(normbias_grad, ("dp", "seq"), scatter_dimension=0, tiled=True),
        lax.psum_scatter(expandmap_grad, ("dp", "seq"), scatter_dimension=0, tiled=True),
        lax.psum_scatter(expandbias_grad, ("dp", "seq"), scatter_dimension=0, tiled=True),
        lax.psum_scatter(shrinkmap_grad, ("dp", "seq"), scatter_dimension=0, tiled=True),
        lax.psum_scatter(shrinkbias_grad, ("dp", "seq"), scatter_dimension=0, tiled=True),
        lax.psum_scatter(outgain_grad, ("dp", "seq"), scatter_dimension=0, tiled=True),
        lax.psum_scatter(outbias_grad, ("dp", "seq"), scatter_dimension=0, tiled=True),
    )
    return (
        layer_out.reshape(seqrows, qlength, width).astype(jnp.bfloat16),
        raw_logits,
        tokens_grad.reshape(seqrows, qlength, width).astype(jnp.bfloat16),
        logits_grad,
    ) + tuple(owned)


def solution(mesh):
    in_specs = (
        P("dp", "seq", None),
        P("dp", None, "seq", None),
        P("dp", None),
        P("dp", "seq", None),
        P("dp", None, "seq", None),
        P(("dp", "seq"), None),
        P(("dp", "seq")),
        P(("dp", "seq"), None),
        P(("dp", "seq"), None),
        P(("dp", "seq")),
        P(("dp", "seq"), None),
        P(("dp", "seq")),
        P(("dp", "seq")),
        P(("dp", "seq")),
        P(("dp", "seq"), None),
        P(("dp", "seq")),
        P(("dp", "seq"), None),
        P(("dp", "seq")),
        P(("dp", "seq")),
        P(("dp", "seq")),
    )
    out_specs = (
        P("dp", "seq", None),
        P("dp", None, "seq", None),
        P("dp", "seq", None),
        P("dp", None, "seq", None),
        P(("dp", "seq"), None),
        P(("dp", "seq")),
        P(("dp", "seq"), None),
        P(("dp", "seq"), None),
        P(("dp", "seq")),
        P(("dp", "seq"), None),
        P(("dp", "seq")),
        P(("dp", "seq")),
        P(("dp", "seq")),
        P(("dp", "seq"), None),
        P(("dp", "seq")),
        P(("dp", "seq"), None),
        P(("dp", "seq")),
        P(("dp", "seq")),
        P(("dp", "seq")),
    )
    return jax.shard_map(body, mesh=mesh, in_specs=in_specs, out_specs=out_specs, check_vma=False)
```

profile of v0, /device:TPU:0, one launch (start us, length us, event | category | flops | bytes accessed | tf_op | source)
XLA Modules:
  0.0 1690.0 jit_solution(7666844894113663365)
XLA Ops:
  17.0 42.5 %all-reduce.28 = (bf16[3072]{0:T(1024)(128)(2,1)S(1)}, bf16[768]{0:T(1024)(128)(2,1)S(1)}, bf16[768]{0:T(1024)(128)(2,1)S(1)}, bf16[768]{0:T(1024)(128)(2,1)S(1)...) all-reduce(bf16[3072]{0:T(1024)(128)(2,1)S(1)} %dynamic-update-slic, ...), channel_id=1, replica_groups=mesh['dp'=16,'seq'=2] {'dp','seq'}, use_global_device_ids=true, to_apply=%add.5 | all-reduce | flops 9216 | bytes 36864
  71.7 51.8 %all-gather.19.cloned.1.call-done = bf16[768,768]{1,0:T(8,128)(2,1)} async-done(((bf16[24,768]{1,0:T(8,128)(2,1)}), bf16[768,768]{1,0:T(8,128)(2,1)}) %all-gather.19.cloned.1.call-update) | async-done | bytes 1179664 | tf_op jit(solution)/shard_map/all_gather | solution.py:69
  130.8 48.5 %all-gather.17.cloned.1.call-done = bf16[768,768]{1,0:T(8,128)(2,1)} async-done(((bf16[24,768]{1,0:T(8,128)(2,1)}), bf16[768,768]{1,0:T(8,128)(2,1)}) %all-gather.17.cloned.1.call-update) | async-done | bytes 1179664 | tf_op jit(solution)/shard_map/all_gather | solution.py:67
  214.1 32.1 %while.40 = (s32[]{:T(128)}, bf16[3,12,256,512]{3,2,1,0:T(8,128)(2,1)}, bf16[3,256,12,64]{1,3,2,0:T(8,128)(2,1)}, bf16[3,12,256,512]{3,2,1,0:T(8,128)(2,1)}, bf1...) while((s32[]{:T(128)}, ...), condition=%wide.region_3.4_spmd, body=%wide.region_0.3_spmd.sunk | while | flops 418578944 | bytes 34237024 | solution.py:135
  248.9 14.2 all-gather.27.cloned.1.call-done
  267.5 61.0 %all-gather.29.cloned.1.call-done = bf16[768,3072]{1,0:T(8,128)(2,1)} async-done(((bf16[24,3072]{1,0:T(8,128)(2,1)}), bf16[768,3072]{1,0:T(8,128)(2,1)}) %all-gather.29.cloned.1.call-update) | async-done | bytes 4718608 | tf_op jit(solution)/shard_map/all_gather | solution.py:76
  328.6 64.9 %all-gather.31.cloned.1.call-done = bf16[3072,768]{1,0:T(8,128)(2,1)} async-done(((bf16[96,768]{1,0:T(8,128)(2,1)}), bf16[3072,768]{1,0:T(8,128)(2,1)}) %all-gather.31.cloned.1.call-update) | async-done | bytes 4718608 | tf_op jit(solution)/shard_map/all_gather | solution.py:78
  393.4 31.3 %fusion.143 = (f32[768]{0:T(1024)S(1)}, f32[768,768]{1,0:T(8,128)S(1)}) fusion(f32[768]{0:T(1024)S(1)} %convert_element_type.242, bf16[3072,768]{1,0:T(8,128)(2,1)} %all-gather.31.cloned.1.call-done, bf16[768,3072]{1,0:T(8,128)(2,1)} %all-gather.29.cloned.1.call-done, f32[3072]{0:T(1024)S(1)} %convert_element_type.240, f32[768,768]{1,0:T(8,128)} %copy-done.20, ...), kind=kOutput, calls=%fused_computation.221 | convolution fusion | flops 7411727360 | bytes 14186496 | tf_op jit(solution)/shard_map/dot_general | solution.py:14
  432.6 39.5 %all-reduce.27 = (bf16[768]{0:T(1024)(128)(2,1)S(1)}, bf16[768]{0:T(1024)(128)(2,1)S(1)}, bf16[768]{0:T(1024)(128)(2,1)S(1)}, bf16[768]{0:T(1024)(128)(2,1)S(1)}...) all-reduce(bf16[768]{0:T(1024)(128)(2,1)S(1)} %dynamic-update-slice, ...), channel_id=1, replica_groups=mesh['dp'=16,'seq'=2] {'dp','seq'}, use_global_device_ids=true, to_apply=%add.10 | all-reduce | flops 8448 | bytes 33792
  483.1 52.2 %all-gather.39.cloned.1.call-done = bf16[768,768]{1,0:T(8,128)(2,1)} async-done(((bf16[24,768]{1,0:T(8,128)(2,1)}), bf16[768,768]{1,0:T(8,128)(2,1)}) %all-gather.39.cloned.1.call-update) | async-done | bytes 1179664 | tf_op jit(solution)/shard_map/all_gather | solution.py:69
  543.0 48.1 %all-gather.37.cloned.1.call-done = bf16[768,768]{1,0:T(8,128)(2,1)} async-done(((bf16[24,768]{1,0:T(8,128)(2,1)}), bf16[768,768]{1,0:T(8,128)(2,1)}) %all-gather.37.cloned.1.call-update) | async-done | bytes 1179664 | tf_op jit(solution)/shard_map/all_gather | solution.py:67
  620.1 31.9 %while.41 = (s32[]{:T(128)}, bf16[3,256,12,64]{1,3,2,0:T(8,128)(2,1)}, f32[3,12,256,1]{2,1,3,0:T(8,128)}, bf16[3,512,12,64]{1,3,2,0:T(8,128)(2,1)}, pred[3,1,256...) while((s32[]{:T(128)}, ...), condition=%wide.region_11.12_spmd, body=%wide.region_8.11_spmd.sunk | while | flops 418575360 | bytes 24878176 | solution.py:135
  655.9 18.1 %all-gather.43.cloned.1.call-done = bf16[768,768]{1,0:T(8,128)(2,1)} async-done(((bf16[24,768]{1,0:T(8,128)(2,1)}), bf16[768,768]{1,0:T(8,128)(2,1)}) %all-gather.43.cloned.1.call-update) | async-done | bytes 1179664 | tf_op jit(solution)/shard_map/all_gather | solution.py:72
  679.2 60.1 %all-gather.45.cloned.1.call-done = bf16[768,3072]{1,0:T(8,128)(2,1)} async-done(((bf16[24,3072]{1,0:T(8,128)(2,1)}), bf16[768,3072]{1,0:T(8,128)(2,1)}) %all-gather.45.cloned.1.call-update) | async-done | bytes 4718608 | tf_op jit(solution)/shard_map/all_gather | solution.py:76
  739.3 28.4 %multiply_convert_fusion = (bf16[768,3072]{1,0:T(8,128)(2,1)}, f32[768,3072]{1,0:T(8,128)}, f32[768,3072]{1,0:T(8,128)}) fusion(f32[3072]{0:T(1024)S(1)} %copy-done.38, bf16[768,3072]{1,0:T(8,128)(2,1)} %all-gather.45.cloned.1.call-done, f32[768,768]{1,0:T(8,128)} %copy-done.6, f32[768]{0:T(1024)S(1)} %convert_element_type.255, ...), kind=kOutput, calls=%fused_computation.89 | convolution fusion | flops 3782541312 | bytes 30695424 | tf_op jit(solution)/shard_map/dot_general | solution.py:14
  767.6 36.4 %all-gather.47.cloned.1.call-done = bf16[3072,768]{1,0:T(8,128)(2,1)} async-done(((bf16[96,768]{1,0:T(8,128)(2,1)}), bf16[3072,768]{1,0:T(8,128)(2,1)}) %all-gather.47.cloned.1.call-update) | async-done | bytes 4718608 | tf_op jit(solution)/shard_map/all_gather | solution.py:78
  855.3 101.8 %while.42 = (s32[]{:T(128)}, bf16[3,12,256,512]{3,2,1,0:T(8,128)(2,1)}, bf16[3,256,12,64]{1,3,2,0:T(8,128)(2,1)}, bf16[3,512,12,64]{1,3,2,0:T(8,128)(2,1)}, bf16...) while((s32[]{:T(128)}, ...), condition=%wide.region_22.23_spmd, body=%wide.region_20.22_spmd.sunk | while | flops 1026100736 | bytes 124696864 | solution.py:315
  1009.9 41.7 %all-reduce.26 = (f32[768]{0:T(1024)S(1)}, f32[768]{0:T(1024)S(1)}, f32[768]{0:T(1024)S(1)}, f32[768]{0:T(1024)S(1)}, f32[768]{0:T(1024)S(1)}, /*index=5*/f32[30...) all-reduce(f32[768]{0:T(1024)S(1)} %reduce_sum.231, ...), channel_id=5, replica_groups=mesh['dp'=16,'seq'=2] {'dp','seq'}, use_global_device_ids=true, to_apply=%region_27.28.clone | all-reduce | flops 9216 | bytes 73728
  1063.6 22.2 %reduce-scatter.19.cloned.1.call-done = f32[24,768]{1,0:T(8,128)} async-done(((f32[768,768]{1,0:T(8,128)}), f32[24,768]{1,0:T(8,128)}) %reduce-scatter.19.cloned.1.call-update) | async-done | bytes 73744 | tf_op jit(solution)/shard_map/reduce_scatter | solution.py:362
  1085.8 104.4 %reduce-scatter.25.cloned.1.call-done = f32[24,768]{1,0:T(8,128)} async-done(((f32[768,768]{1,0:T(8,128)}), f32[24,768]{1,0:T(8,128)}) %reduce-scatter.25.cloned.1.call-update) | async-done | bytes 73744
  1190.2 104.5 %reduce-scatter.27.cloned.1.call-done = f32[24,768]{1,0:T(8,128)} async-done(((f32[768,768]{1,0:T(8,128)}), f32[24,768]{1,0:T(8,128)}) %reduce-scatter.27.cloned.1.call-update) | async-done | bytes 73744
  1294.7 104.5 %reduce-scatter.29.cloned.1.call-done = f32[24,768]{1,0:T(8,128)} async-done(((f32[768,768]{1,0:T(8,128)}), f32[24,768]{1,0:T(8,128)}) %reduce-scatter.29.cloned.1.call-update) | async-done | bytes 73744
  1399.3 142.0 %reduce-scatter.23.cloned.1.call-done = f32[96,768]{1,0:T(8,128)} async-done(((f32[3072,768]{1,0:T(8,128)}), f32[96,768]{1,0:T(8,128)}) %reduce-scatter.23.cloned.1.call-update) | async-done | bytes 294928 | tf_op jit(solution)/shard_map/reduce_scatter | solution.py:368
  1541.2 141.7 %reduce-scatter.21.cloned.1.call-done = f32[24,3072]{1,0:T(8,128)} async-done(((f32[768,3072]{1,0:T(8,128)}), f32[24,3072]{1,0:T(8,128)}) %reduce-scatter.21.cloned.1.call-update) | async-done | bytes 294928 | tf_op jit(solution)/shard_map/reduce_scatter | solution.py:366
  (367 shorter events, 416.4 us)
Async XLA Ops:
  7.2 60.6 %all-gather.23.cloned.1.call-start = ((), (), s32[]{:S(2)}) async-start(), calls=%async_computation.11 | async-start | bytes 1216512 | tf_op jit(solution)/shard_map/all_gather | solution.py:70
  7.9 115.6 %all-gather.19.cloned.1.call-start = ((), (), s32[]{:S(2)}) async-start(), calls=%async_computation.9 | async-start | bytes 1216512 | tf_op jit(solution)/shard_map/all_gather | solution.py:69
  8.7 170.6 %all-gather.17.cloned.1.call-start = ((), (), s32[]{:S(2)}) async-start(), calls=%async_computation.8 | async-start | bytes 1216512 | tf_op jit(solution)/shard_map/all_gather | solution.py:67
  9.4 181.7 %all-gather.25.cloned.1.call-start = ((), (), s32[]{:S(2)}) async-start(), calls=%async_computation.12 | async-start | bytes 3538944 | tf_op jit(solution)/shard_map/all_gather | solution.py:111
  71.7 133.6 %all-gather.21.cloned.1.call-start = ((), (), s32[]{:S(2)}) async-start(), calls=%async_computation.10 | async-start | bytes 3538944 | tf_op jit(solution)/shard_map/all_gather | solution.py:110
  126.9 136.2 %all-gather.27.cloned.1.call-start = ((), (), s32[]{:S(2)}) async-start(), calls=%async_computation.13 | async-start | bytes 1216512 | tf_op jit(solution)/shard_map/all_gather | solution.py:72
  127.5 201.1 %all-gather.29.cloned.1.call-start = ((), (), s32[]{:S(2)}) async-start(), calls=%async_computation.14 | async-start | bytes 4866048 | tf_op jit(solution)/shard_map/all_gather | solution.py:76
  128.2 265.2 %all-gather.31.cloned.1.call-start = ((), (), s32[]{:S(2)}) async-start(), calls=%async_computation.15 | async-start | bytes 4866048 | tf_op jit(solution)/shard_map/all_gather | solution.py:78
  129.0 350.7 %all-gather.33.cloned.1.call-start = ((), (), s32[]{:S(2)}) async-start(), calls=%async_computation.16 | async-start | bytes 1216512 | tf_op jit(solution)/shard_map/all_gather | solution.py:70
  426.9 108.4 %all-gather.39.cloned.1.call-start = ((), (), s32[]{:S(2)}) async-start(), calls=%async_computation.19 | async-start | bytes 1216512 | tf_op jit(solution)/shard_map/all_gather | solution.py:69
  427.5 163.5 %all-gather.37.cloned.1.call-start = ((), (), s32[]{:S(2)}) async-start(), calls=%async_computation.18 | async-start | bytes 1216512 | tf_op jit(solution)/shard_map/all_gather | solution.py:67
  428.3 174.1 %all-gather.35.cloned.1.call-start = ((), (), s32[]{:S(2)}) async-start(), calls=%async_computation.17 | async-start | bytes 3538944 | tf_op jit(solution)/shard_map/all_gather | solution.py:111
  483.1 133.0 %all-gather.41.cloned.1.call-start = ((), (), s32[]{:S(2)}) async-start(), calls=%async_computation.20 | async-start | bytes 3538944 | tf_op jit(solution)/shard_map/all_gather | solution.py:110
  538.7 135.2 %all-gather.43.cloned.1.call-start = ((), (), s32[]{:S(2)}) async-start(), calls=%async_computation.21 | async-start | bytes 1216512 | tf_op jit(solution)/shard_map/all_gather | solution.py:72
  539.3 199.9 %all-gather.45.cloned.1.call-start = ((), (), s32[]{:S(2)}) async-start(), calls=%async_computation.22 | async-start | bytes 4866048 | tf_op jit(solution)/shard_map/all_gather | solution.py:76
  539.9 264.1 %all-gather.47.cloned.1.call-start = ((), (), s32[]{:S(2)}) async-start(), calls=%async_computation.23 | async-start | bytes 4866048 | tf_op jit(solution)/shard_map/all_gather | solution.py:78
  542.9 425.5 %reduce-scatter.15.cloned.1.call-start = ((), (), s32[]{:S(2)}) async-start(), calls=%async_computation.24 | async-start | bytes 3538944 | tf_op jit(solution)/shard_map/reduce_scatter | solution.py:329
  957.1 21.7 %reduce-scatter.17.cloned.1.call-start = ((), (), s32[]{:S(2)}) async-start(), calls=%async_computation.25 | async-start | bytes 3538944 | tf_op jit(solution)/shard_map/reduce_scatter | solution.py:335
  957.7 128.1 %reduce-scatter.19.cloned.1.call-start = ((), (), s32[]{:S(2)}) async-start(), calls=%async_computation.26 | async-start | bytes 2433024 | tf_op jit(solution)/shard_map/reduce_scatter | solution.py:362
  961.6 228.6 %reduce-scatter.25.cloned.1.call-start = ((), (), s32[]{:S(2)}) async-start(), calls=%async_computation.29 | async-start | bytes 2433024
  968.4 326.4 %reduce-scatter.27.cloned.1.call-start = ((), (), s32[]{:S(2)}) async-start(), calls=%async_computation.30 | async-start | bytes 2433024
  973.2 426.1 %reduce-scatter.29.cloned.1.call-start = ((), (), s32[]{:S(2)}) async-start(), calls=%async_computation.31 | async-start | bytes 2433024
  983.6 557.6 %reduce-scatter.23.cloned.1.call-start = ((), (), s32[]{:S(2)}) async-start(), calls=%async_computation.28 | async-start | bytes 9732096 | tf_op jit(solution)/shard_map/reduce_scatter | solution.py:368
  994.2 688.8 %reduce-scatter.21.cloned.1.call-start = ((), (), s32[]{:S(2)}) async-start(), calls=%async_computation.27 | async-start | bytes 9732096 | tf_op jit(solution)/shard_map/reduce_scatter | solution.py:366
  (62 other events, 1012.8 us)
Sparse Core Ops, SparseCore 0:
  10.9 56.8 all-gather.22
  70.7 52.7 all-gather.18
  126.4 52.8 all-gather.16
  181.2 9.8 all-gather.24
  193.1 12.1 all-gather.20
  208.0 55.0 all-gather.26
  266.0 62.4 all-gather.28
  331.5 61.9 all-gather.30
  427.1 52.5 all-gather.32
  482.4 52.8 all-gather.38
  538.2 52.8 all-gather.36
  592.5 9.8 all-gather.34
  603.9 12.1 all-gather.40
  618.8 55.1 all-gather.42
  676.7 62.4 all-gather.44
  742.0 61.9 all-gather.46
  957.2 8.2 reduce-scatter.14
  967.6 11.1 reduce-scatter.16
  984.7 101.0 reduce-scatter.18
  1091.5 98.6 reduce-scatter.24
  1196.1 98.6 reduce-scatter.26
  1300.6 98.6 reduce-scatter.28
  1405.7 135.4 reduce-scatter.22
  1547.5 135.3 reduce-scatter.20
where the time goes:
time: 1700 us; the launch traced here: 1690 us
  waiting for transfers between devices  1130 us (66%)
  matrix products  260 us (15%)
  blocking collectives  124 us (7%)
  local copies, waits for them, and re-layouts  102 us (6%)
  other arithmetic  62.3 us (4%)
    unnamed x27, waiting for transfers between devices  320 us
    reduce_scatter x1, waiting for transfers between devices, body(): lax.psum_scatter(shrinkmap_grad, ('dp', 'seq'), scatter_dimension=0, tile...  142 us
    reduce_scatter x1, waiting for transfers between devices, body(): lax.psum_scatter(expandmap_grad, ('dp', 'seq'), scatter_dimension=0, tile...  142 us
    unnamed x3, blocking collectives  124 us
    all_gather x2, waiting for transfers between devices, forward(): lax.all_gather(expandmap, ('dp', 'seq'), axis=0, tiled=True)  121 us
    all_gather x2, waiting for transfers between devices, forward(): lax.all_gather(keymap, ('dp', 'seq'), axis=0, tiled=True)  104 us
    all_gather x2, waiting for transfers between devices, forward(): lax.all_gather(shrinkmap, ('dp', 'seq'), axis=0, tiled=True)  101 us
    all_gather x2, waiting for transfers between devices, forward(): lax.all_gather(querymap, ('dp', 'seq'), axis=0, tiled=True)  96.6 us
  transfers between devices with their start and end apart: 24, of which 23 were waited for; matrix products, arithmetic and copies ran while one was open for 13% of the time, Pallas kernels for 0%

commit v1 on v0

--- a/solution.py
+++ b/solution.py
@@ -8,6 +8,18 @@
 HD = 64
 norm_eps = 1e-06
 mask_fill = -1e30
+
+
+def gather_by_bits(x, axis, dim):
+    ways, here = (lax.axis_size(axis), lax.axis_index(axis))
+    grown, reach = (x, 1)
+    while reach < ways:
+        theirs = lax.ppermute(grown, axis, [(d, d ^ reach) for d in range(ways)])
+        mine_first = jnp.concatenate([grown, theirs], axis=dim)
+        theirs_first = jnp.concatenate([theirs, grown], axis=dim)
+        grown = jnp.where(here & reach == 0, mine_first, theirs_first)
+        reach = 2 * reach
+    return grown
 
 
 def matmul(left_side, right_side):
@@ -73,7 +85,7 @@
         lax.all_gather(mixbias, ("dp", "seq"), axis=0, tiled=True),
         lax.all_gather(normgain, ("dp", "seq"), axis=0, tiled=True),
         lax.all_gather(normbias, ("dp", "seq"), axis=0, tiled=True),
-        lax.all_gather(expandmap, ("dp", "seq"), axis=0, tiled=True),
+        gather_by_bits(expandmap, ("dp", "seq"), 0),
         lax.all_gather(expandbias, ("dp", "seq"), axis=0, tiled=True),
         lax.all_gather(shrinkmap, ("dp", "seq"), axis=0, tiled=True),
         lax.all_gather(shrinkbias, ("dp", "seq"), axis=0, tiled=True),

time: 1700 us -> 1640 us (0.965)
  waiting for transfers between devices: 1130 us -> 1040 us
    all_gather x2 -> x0, waiting for transfers between devices: 121 us -> none  [forward(): lax.all_gather(expandmap, ('dp', 'seq'), axis=0, tiled=True)]
    all_gather x2, waiting for transfers between devices: 96.6 us -> 0.01 us  [forward(): lax.all_gather(querymap, ('dp', 'seq'), axis=0, tiled=True)]
    ppermute x0 -> x10, waiting for transfers between devices: none -> 96.2 us  [gather_by_bits(): theirs = lax.ppermute(grown, axis, [(d, d ^ reach) for d in range(ways)])]
    all_gather x2, waiting for transfers between devices: 32.3 us -> 123 us  [forward(): lax.all_gather(mixmap, ('dp', 'seq'), axis=0, tiled=True)]
    all_gather x2, waiting for transfers between devices: 101 us -> 65 us  [forward(): lax.all_gather(shrinkmap, ('dp', 'seq'), axis=0, tiled=True)]
    dot_general x11 -> x12, matrix products: 93.1 us -> 99.6 us  [matmul(): return jnp.dot(left_side, right_side, preferred_element_type=jnp.float32)]
    unnamed x27 -> x25, waiting for transfers between devices: 320 us -> 317 us
    unnamed x143 -> x157, local copies, waits for them, and re-layouts: 37.7 us -> 34.8 us
  transfers between devices with their start and end apart: 24 -> 32, of which waited for: 23 -> 25; matrix products, arithmetic and copies ran while one was open for 13% -> 16% of each run, Pallas kernels for 0% -> 0%
where the time goes in v1:
time: 1640 us; the launch traced here: 1630 us
  waiting for transfers between devices  1040 us (63%)
  matrix products  268 us (16%)
  blocking collectives  124 us (8%)
  local copies, waits for them, and re-layouts  99.1 us (6%)
  other arithmetic  71.5 us (4%)
    unnamed x25, waiting for transfers between devices  317 us
    reduce_scatter x1, waiting for transfers between devices, body(): lax.psum_scatter(shrinkmap_grad, ('dp', 'seq'), scatter_dimension=0, tile...  142 us
    reduce_scatter x1, waiting for transfers between devices, body(): lax.psum_scatter(expandmap_grad, ('dp', 'seq'), scatter_dimension=0, tile...  142 us
    unnamed x3, blocking collectives  124 us
    all_gather x2, waiting for transfers between devices, forward(): lax.all_gather(mixmap, ('dp', 'seq'), axis=0, tiled=True)  123 us
    all_gather x2, waiting for transfers between devices, forward(): lax.all_gather(keymap, ('dp', 'seq'), axis=0, tiled=True)  104 us
    dot_general x12, matrix products, matmul(): return jnp.dot(left_side, right_side, preferred_element_type=jnp.float32)  99.6 us
    ppermute x10, waiting for transfers between devices, gather_by_bits(): theirs = lax.ppermute(grown, axis, [(d, d ^ reach) for d in range(ways)])  96.2 us
  transfers between devices with their start and end apart: 32, of which 25 were waited for; matrix products, arithmetic and copies ran while one was open for 16% of the time, Pallas kernels for 0%

profile of v1, /device:TPU:0, one launch (start us, length us, event | category | flops | bytes accessed | tf_op | source)
XLA Modules:
  0.0 1630.1 jit_solution(7687420342198875384)
XLA Ops:
  17.0 42.5 %all-reduce.28 = (bf16[3072]{0:T(1024)(128)(2,1)S(1)}, bf16[768]{0:T(1024)(128)(2,1)S(1)}, bf16[768]{0:T(1024)(128)(2,1)S(1)}, bf16[768]{0:T(1024)(128)(2,1)S(1)...) all-reduce(bf16[3072]{0:T(1024)(128)(2,1)S(1)} %dynamic-update-slic, ...), channel_id=1, replica_groups=mesh['dp'=16,'seq'=2] {'dp','seq'}, use_global_device_ids=true, to_apply=%add.5 | all-reduce | flops 9216 | bytes 36864
  71.7 51.8 %all-gather.17.cloned.1.call-done = bf16[768,768]{1,0:T(8,128)(2,1)} async-done(((bf16[24,768]{1,0:T(8,128)(2,1)}), bf16[768,768]{1,0:T(8,128)(2,1)}) %all-gather.17.cloned.1.call-update) | async-done | bytes 1179664 | tf_op jit(solution)/shard_map/all_gather | solution.py:81
  139.6 13.6 collective-permute-done.2
  156.0 27.6 %collective-permute-done.3 = bf16[192,3072]{1,0:T(8,128)(2,1)S(1)} collective-permute-done((bf16[192,3072]{1,0:T(8,128)(2,1)S(1)}, bf16[192,3072]{1,0:T(8,128)(2,1)S(1)}, u32[]{:S(2)}, u32[]{:S(2)}) %collective-permute-start.3) | collective-permute-done | bytes 1179680 | tf_op jit(solution)/shard_map/ppermute | solution.py:17
  214.5 32.1 %while.40 = (s32[]{:T(128)}, bf16[3,12,256,512]{3,2,1,0:T(8,128)(2,1)}, bf16[3,256,12,64]{1,3,2,0:T(8,128)(2,1)}, bf16[3,12,256,512]{3,2,1,0:T(8,128)(2,1)}, bf1...) while((s32[]{:T(128)}, ...), condition=%wide.region_3.4_spmd, body=%wide.region_0.3_spmd.sunk | while | flops 418578944 | bytes 34237024 | solution.py:147
  250.3 58.6 %all-gather.25.cloned.1.call-done = bf16[768,768]{1,0:T(8,128)(2,1)} async-done(((bf16[24,768]{1,0:T(8,128)(2,1)}), bf16[768,768]{1,0:T(8,128)(2,1)}) %all-gather.25.cloned.1.call-update) | async-done | bytes 1179664 | tf_op jit(solution)/shard_map/all_gather | solution.py:84
  312.6 27.4 %fusion.69.clone.3.clone.4 = bf16[768,3072]{1,0:T(8,128)(2,1)} fusion(bf16[384,3072]{1,0:T(8,128)(2,1)} %collective-permute-done.4, bf16[384,3072]{1,0:T(8,128)(2,1)} %maximum_select_fusion.5, f32[3072]{0:T(1024)S(1)} %convert_element_type.240, pred[]{:T(512)S(6)} %eq.43, f32[768,768]{1,0:T(8,128)S(1)} %get-tuple-element.516, ...), kind=kOutput, calls=%fused_computation.85.clone.clone.clone.clone.clone.clone.clone.1 | convolution fusion | flops 3803774976 | bytes 11821057 | tf_op jit(solution)/shard_map/dot_general | solution.py:26
  340.1 34.3 %all-gather.27.cloned.1.call-done = bf16[3072,768]{1,0:T(8,128)(2,1)} async-done(((bf16[96,768]{1,0:T(8,128)(2,1)}), bf16[3072,768]{1,0:T(8,128)(2,1)}) %all-gather.27.cloned.1.call-update) | async-done | bytes 4718608 | tf_op jit(solution)/shard_map/all_gather | solution.py:90
  387.6 39.7 %all-reduce.27 = (bf16[768]{0:T(1024)(128)(2,1)}, bf16[768]{0:T(1024)(128)(2,1)S(1)}, bf16[768]{0:T(1024)(128)(2,1)}, bf16[768]{0:T(1024)(128)(2,1)}, bf16[768]{...) all-reduce(bf16[768]{0:T(1024)(128)(2,1)S(1)} %dynamic-update-slice, ...), channel_id=1, replica_groups=mesh['dp'=16,'seq'=2] {'dp','seq'}, use_global_device_ids=true, to_apply=%add.10 | all-reduce | flops 8448 | bytes 33792
  439.8 52.3 %all-gather.35.cloned.1.call-done = bf16[768,768]{1,0:T(8,128)(2,1)} async-done(((bf16[24,768]{1,0:T(8,128)(2,1)}), bf16[768,768]{1,0:T(8,128)(2,1)}) %all-gather.35.cloned.1.call-update) | async-done | bytes 1179664 | tf_op jit(solution)/shard_map/all_gather | solution.py:81
  508.2 13.7 collective-permute-done.7
  529.1 23.2 %collective-permute-done.8 = bf16[192,3072]{1,0:T(8,128)(2,1)S(1)} collective-permute-done((bf16[192,3072]{1,0:T(8,128)(2,1)S(1)}, bf16[192,3072]{1,0:T(8,128)(2,1)S(1)}, u32[]{:S(2)}, u32[]{:S(2)}) %collective-permute-start.8) | collective-permute-done | bytes 1179680 | tf_op jit(solution)/shard_map/ppermute | solution.py:17
  577.1 31.9 %while.41 = (s32[]{:T(128)}, bf16[3,256,12,64]{1,3,2,0:T(8,128)(2,1)}, f32[3,12,256,1]{2,1,3,0:T(8,128)}, bf16[3,512,12,64]{1,3,2,0:T(8,128)(2,1)}, pred[3,1,256...) while((s32[]{:T(128)}, ...), condition=%wide.region_11.12_spmd, body=%wide.region_8.11_spmd.sunk | while | flops 418575360 | bytes 24878176 | solution.py:147
  613.0 64.8 %all-gather.39.cloned.1.call-done = bf16[768,768]{1,0:T(8,128)(2,1)} async-done(((bf16[24,768]{1,0:T(8,128)(2,1)}), bf16[768,768]{1,0:T(8,128)(2,1)}) %all-gather.39.cloned.1.call-update) | async-done | bytes 1179664 | tf_op jit(solution)/shard_map/all_gather | solution.py:84
  682.5 29.9 %multiply_convert_fusion = (bf16[768,3072]{1,0:T(8,128)(2,1)}, f32[768,3072]{1,0:T(8,128)}, f32[768,3072]{1,0:T(8,128)}) fusion(f32[3072]{0:T(1024)S(1)} %copy-done.39, bf16[384,3072]{1,0:T(8,128)(2,1)} %collective-permute-done.9, bf16[384,3072]{1,0:T(8,128)(2,1)} %maximum_select_fusion.6, pred[]{:T(512)S(6)} %eq.43, ...), kind=kOutput, calls=%fused_computation.89 | convolution fusion | flops 3803774976 | bytes 30695424 | tf_op jit(solution)/shard_map/dot_general | solution.py:26
  712.4 30.7 %all-gather.41.cloned.1.call-done = bf16[3072,768]{1,0:T(8,128)(2,1)} async-done(((bf16[96,768]{1,0:T(8,128)(2,1)}), bf16[3072,768]{1,0:T(8,128)(2,1)}) %all-gather.41.cloned.1.call-update) | async-done | bytes 4718608 | tf_op jit(solution)/shard_map/all_gather | solution.py:90
  796.2 101.8 %while.42 = (s32[]{:T(128)}, bf16[3,12,256,512]{3,2,1,0:T(8,128)(2,1)}, bf16[3,256,12,64]{1,3,2,0:T(8,128)(2,1)}, bf16[3,512,12,64]{1,3,2,0:T(8,128)(2,1)}, bf16...) while((s32[]{:T(128)}, ...), condition=%wide.region_22.23_spmd, body=%wide.region_20.22_spmd.sunk | while | flops 1026100736 | bytes 124696864 | solution.py:327
  950.7 41.7 %all-reduce.26 = (f32[768]{0:T(1024)S(1)}, f32[768]{0:T(1024)S(1)}, f32[768]{0:T(1024)S(1)}, f32[768]{0:T(1024)S(1)}, f32[768]{0:T(1024)S(1)}, /*index=5*/f32[30...) all-reduce(f32[768]{0:T(1024)S(1)} %reduce_sum.231, ...), channel_id=5, replica_groups=mesh['dp'=16,'seq'=2] {'dp','seq'}, use_global_device_ids=true, to_apply=%region_27.28.clone | all-reduce | flops 9216 | bytes 73728
  1004.4 22.0 %reduce-scatter.19.cloned.1.call-done = f32[24,768]{1,0:T(8,128)} async-done(((f32[768,768]{1,0:T(8,128)}), f32[24,768]{1,0:T(8,128)}) %reduce-scatter.19.cloned.1.call-update) | async-done | bytes 73744 | tf_op jit(solution)/shard_map/reduce_scatter | solution.py:374
  1026.5 104.3 %reduce-scatter.25.cloned.1.call-done = f32[24,768]{1,0:T(8,128)} async-done(((f32[768,768]{1,0:T(8,128)}), f32[24,768]{1,0:T(8,128)}) %reduce-scatter.25.cloned.1.call-update) | async-done | bytes 73744
  1130.8 104.5 %reduce-scatter.27.cloned.1.call-done = f32[24,768]{1,0:T(8,128)} async-done(((f32[768,768]{1,0:T(8,128)}), f32[24,768]{1,0:T(8,128)}) %reduce-scatter.27.cloned.1.call-update) | async-done | bytes 73744
  1235.3 104.4 %reduce-scatter.29.cloned.1.call-done = f32[24,768]{1,0:T(8,128)} async-done(((f32[768,768]{1,0:T(8,128)}), f32[24,768]{1,0:T(8,128)}) %reduce-scatter.29.cloned.1.call-update) | async-done | bytes 73744
  1339.7 141.7 %reduce-scatter.23.cloned.1.call-done = f32[96,768]{1,0:T(8,128)} async-done(((f32[3072,768]{1,0:T(8,128)}), f32[96,768]{1,0:T(8,128)}) %reduce-scatter.23.cloned.1.call-update) | async-done | bytes 294928 | tf_op jit(solution)/shard_map/reduce_scatter | solution.py:380
  1481.4 141.6 %reduce-scatter.21.cloned.1.call-done = f32[24,3072]{1,0:T(8,128)} async-done(((f32[768,3072]{1,0:T(8,128)}), f32[24,3072]{1,0:T(8,128)}) %reduce-scatter.21.cloned.1.call-update) | async-done | bytes 294928 | tf_op jit(solution)/shard_map/reduce_scatter | solution.py:378
  (404 shorter events, 444.1 us)
Async XLA Ops:
  7.2 60.6 %all-gather.21.cloned.1.call-start = ((), (), s32[]{:S(2)}) async-start(), calls=%async_computation.11 | async-start | bytes 1216512 | tf_op jit(solution)/shard_map/all_gather | solution.py:82
  7.9 115.6 %all-gather.17.cloned.1.call-start = ((), (), s32[]{:S(2)}) async-start(), calls=%async_computation.9 | async-start | bytes 1216512 | tf_op jit(solution)/shard_map/all_gather | solution.py:81
  8.7 177.9 %all-gather.15.cloned.1.call-start = ((), (), s32[]{:S(2)}) async-start(), calls=%async_computation.8 | async-start | bytes 1216512 | tf_op jit(solution)/shard_map/all_gather | solution.py:79
  9.4 187.9 %all-gather.23.cloned.1.call-start = ((), (), s32[]{:S(2)}) async-start(), calls=%async_computation.12 | async-start | bytes 3538944 | tf_op jit(solution)/shard_map/all_gather | solution.py:123
  71.7 134.0 %all-gather.19.cloned.1.call-start = ((), (), s32[]{:S(2)}) async-start(), calls=%async_computation.10 | async-start | bytes 3538944 | tf_op jit(solution)/shard_map/all_gather | solution.py:122
  126.9 182.0 %all-gather.25.cloned.1.call-start = ((), (), s32[]{:S(2)}) async-start(), calls=%async_computation.13 | async-start | bytes 1216512 | tf_op jit(solution)/shard_map/all_gather | solution.py:84
  130.0 244.3 %all-gather.27.cloned.1.call-start = ((), (), s32[]{:S(2)}) async-start(), calls=%async_computation.14 | async-start | bytes 4866048 | tf_op jit(solution)/shard_map/all_gather | solution.py:90
  153.6 282.6 %all-gather.29.cloned.1.call-start = ((), (), s32[]{:S(2)}) async-start(), calls=%async_computation.15 | async-start | bytes 1216512 | tf_op jit(solution)/shard_map/all_gather | solution.py:82
  185.5 127.1 %collective-permute-start.4 = (bf16[384,3072]{1,0:T(8,128)(2,1)}, bf16[384,3072]{1,0:T(8,128)(2,1)}, u32[]{:S(2)}, u32[]{:S(2)}) collective-permute-start(bf16[384,3072]{1,0:T(8,128)(2,1)} %maximum_select_fusion.5), channel_id=1, source_target_pairs={{0,16},{1,17},{2,18},{3,19},{4,20},{5,21},{6,22},{7,23},{8,24},{9,... | collective-permute-start | bytes 7077896 | tf_op jit(solution)/shard_map/ppermute | solution.py:17
  383.9 108.2 %all-gather.35.cloned.1.call-start = ((), (), s32[]{:S(2)}) async-start(), calls=%async_computation.18 | async-start | bytes 1216512 | tf_op jit(solution)/shard_map/all_gather | solution.py:81
  384.6 170.6 %all-gather.33.cloned.1.call-start = ((), (), s32[]{:S(2)}) async-start(), calls=%async_computation.17 | async-start | bytes 1216512 | tf_op jit(solution)/shard_map/all_gather | solution.py:79
  385.2 180.0 %all-gather.31.cloned.1.call-start = ((), (), s32[]{:S(2)}) async-start(), calls=%async_computation.16 | async-start | bytes 3538944 | tf_op jit(solution)/shard_map/all_gather | solution.py:123
  439.7 133.4 %all-gather.37.cloned.1.call-start = ((), (), s32[]{:S(2)}) async-start(), calls=%async_computation.19 | async-start | bytes 3538944 | tf_op jit(solution)/shard_map/all_gather | solution.py:122
  495.5 182.3 %all-gather.39.cloned.1.call-start = ((), (), s32[]{:S(2)}) async-start(), calls=%async_computation.20 | async-start | bytes 1216512 | tf_op jit(solution)/shard_map/all_gather | solution.py:84
  498.6 244.4 %all-gather.41.cloned.1.call-start = ((), (), s32[]{:S(2)}) async-start(), calls=%async_computation.21 | async-start | bytes 4866048 | tf_op jit(solution)/shard_map/all_gather | solution.py:90
  522.1 30.2 %collective-permute-start.8 = (bf16[192,3072]{1,0:T(8,128)(2,1)S(1)}, bf16[192,3072]{1,0:T(8,128)(2,1)S(1)}, u32[]{:S(2)}, u32[]{:S(2)}) collective-permute-start(bf16[192,3072]{1,0:T(8,128)(2,1)S(1)} %maximum_select_fusion.10), channel_id=1, source_target_pairs={{0,8},{1,9},{2,10},{3,11},{4,12},{5,13},{6,14},{7,15},{8,0},{9,1},... | collective-permute-start | bytes 3538952 | tf_op jit(solution)/shard_map/ppermute | solution.py:17
  529.1 380.5 %reduce-scatter.15.cloned.1.call-start = ((), (), s32[]{:S(2)}) async-start(), calls=%async_computation.22 | async-start | bytes 3538944 | tf_op jit(solution)/shard_map/reduce_scatter | solution.py:341
  554.4 127.0 %collective-permute-start.9 = (bf16[384,3072]{1,0:T(8,128)(2,1)}, bf16[384,3072]{1,0:T(8,128)(2,1)}, u32[]{:S(2)}, u32[]{:S(2)}) collective-permute-start(bf16[384,3072]{1,0:T(8,128)(2,1)} %maximum_select_fusion.6), channel_id=1, source_target_pairs={{0,16},{1,17},{2,18},{3,19},{4,20},{5,21},{6,22},{7,23},{8,24},{9,... | collective-permute-start | bytes 7077896 | tf_op jit(solution)/shard_map/ppermute | solution.py:17
  898.6 127.9 %reduce-scatter.19.cloned.1.call-start = ((), (), s32[]{:S(2)}) async-start(), calls=%async_computation.24 | async-start | bytes 2433024 | tf_op jit(solution)/shard_map/reduce_scatter | solution.py:374
  902.5 228.3 %reduce-scatter.25.cloned.1.call-start = ((), (), s32[]{:S(2)}) async-start(), calls=%async_computation.27 | async-start | bytes 2433024
  909.3 326.0 %reduce-scatter.27.cloned.1.call-start = ((), (), s32[]{:S(2)}) async-start(), calls=%async_computation.28 | async-start | bytes 2433024
  914.3 425.4 %reduce-scatter.29.cloned.1.call-start = ((), (), s32[]{:S(2)}) async-start(), calls=%async_computation.29 | async-start | bytes 2433024
  924.5 556.9 %reduce-scatter.23.cloned.1.call-start = ((), (), s32[]{:S(2)}) async-start(), calls=%async_computation.26 | async-start | bytes 9732096 | tf_op jit(solution)/shard_map/reduce_scatter | solution.py:380
  935.0 688.1 %reduce-scatter.21.cloned.1.call-start = ((), (), s32[]{:S(2)}) async-start(), calls=%async_computation.25 | async-start | bytes 9732096 | tf_op jit(solution)/shard_map/reduce_scatter | solution.py:378
  (77 other events, 1137.5 us)
Sparse Core Ops, SparseCore 0:
  10.9 56.8 all-gather.20
  70.7 52.7 all-gather.16
  126.4 53.2 all-gather.14
  181.7 9.7 all-gather.22
  193.5 12.1 all-gather.18
  208.4 100.4 all-gather.24
  311.8 62.5 all-gather.26
  384.0 52.1 all-gather.28
  439.1 52.8 all-gather.34
  494.8 53.3 all-gather.32
  549.7 9.7 all-gather.30
  560.9 12.1 all-gather.36
  576.0 101.7 all-gather.38
  680.5 62.4 all-gather.40
  898.1 8.2 reduce-scatter.14
  908.5 11.2 reduce-scatter.16
  925.5 100.9 reduce-scatter.18
  1032.2 98.5 reduce-scatter.24
  1136.7 98.5 reduce-scatter.26
  1241.0 98.6 reduce-scatter.28
  1346.1 135.2 reduce-scatter.22
  1487.9 135.1 reduce-scatter.20
